TPU v7x, 32 devices: a whole 2x2x4 slice. The times are simulated.
32 devices in a mesh: gx: 8 (over z, core), gy: 4 (over y, x).
Axes of the slice: x: 2, y: 2, z: 4, core: 2. Of those that a mesh axis runs over, the one named last changes fastest.
Arguments:
- ensemble: float32 [80, 192, 512], P(None, 'gx', 'gy'), may hold values from -6 to 6
- obs_values: float32 [3, 1024], replicated, may hold values from -8 to 8
- obs_error: float32 [3, 1024], replicated, may hold values from 0.2 to 2
- obs_cell: int32 [3, 1024], replicated, may hold values from 0 to 3071
- band_offsets: int32 [3], replicated, may hold values from 24 to 71
Outputs:
- analysis: float32 [80, 192, 512], P(None, 'gx', 'gy')
Inputs may be any that keep to these rules, and one draw needn't show every extreme that they name: `obs_cell`: an observation of device p lies in p's own tile.
All inputs are finite; a program needn't handle non-finite values.
Results may differ from a plain program's by a relative error of at most 0.011.
Values sent between devices are 32-bit elements; how exact they have to be, the bound alone decides.
No kernel may reach another device: no remote copies, remote signals or barrier semaphores. Data moves between devices by JAX's collectives and lax.ppermute only.
A program may use at most 64 MiB of HBM per device.

v0:
```python
import math

import jax
import jax.numpy as jnp
from jax import lax
from jax.sharding import PartitionSpec as P

LEVELS = 8
CY = 16
CX = 24
OBS_DEV = 32
BATCHES = 3


def taper(distance, radius):
    ratio = distance / radius
    return jnp.where(ratio < 1.0, (1.0 - ratio) ** 2 * (1.0 + 2.0 * ratio), 0.0)


def locate(obs_index, cell_ids, gy_count):
    owner = obs_index // OBS_DEV
    column_len = CY * LEVELS
    obs_x = owner // gy_count * CX + cell_ids // column_len
    obs_y = owner % gy_count * CY + cell_ids % column_len // LEVELS
    return (obs_x, obs_y)


def statistics(panel_now, errors, values):
    members = panel_now.shape[0]
    obs_mean = jnp.mean(panel_now, axis=0)
    deviate = panel_now - obs_mean
    variance = jnp.sum(deviate * deviate, axis=0) / (members - 1)
    total_var = variance + errors
    scaling = 1.0 / ((members - 1) * total_var)
    shrink = 1.0 / (1.0 + jnp.sqrt(errors / total_var))
    weighted = jnp.concatenate([shrink * deviate, (values - obs_mean)[None, :]], axis=0).astype(
        jnp.bfloat16
    )
    return (deviate.astype(jnp.bfloat16), scaling, weighted)


def update_cells(columns, cell_x, cell_y, obs_x, obs_y, radius, extent, packed):
    pert_obs, scaling, weighted = packed
    members = columns.shape[0]
    ens_mean = jnp.mean(columns, axis=0)
    spread = columns - ens_mean
    covar = lax.dot_general(
        spread.astype(jnp.bfloat16),
        pert_obs,
        (((0,), (0,)), ((), ())),
        preferred_element_type=jnp.float32,
    )
    gap_x = jnp.abs(cell_x[:, None] - obs_x[None, :])
    gap_x = jnp.minimum(gap_x, extent - gap_x)
    gap_y = jnp.abs(cell_y[:, None] - obs_y[None, :])
    weights = taper(gap_x.astype(jnp.float32), radius) * taper(gap_y.astype(jnp.float32), radius)
    gain_wts = (weights * covar * scaling[None, :]).astype(jnp.bfloat16)
    increment = lax.dot_general(
        weighted, gain_wts, (((1,), (1,)), ((), ())), preferred_element_type=jnp.float32
    )
    return ens_mean + increment[members] + spread - increment[:members]


def per_device(ensemble, obs_values, obs_error, obs_cell, band_offsets):
    members, rows_here, row_len = ensemble.shape
    gx_count = lax.axis_size("gx")
    gy_count = lax.axis_size("gy")
    gx_pos = lax.axis_index("gx")
    gy_pos = lax.axis_index("gy")
    device = gx_pos * gy_count + gy_pos
    extent = CX * gx_count
    total_cells = rows_here * row_len
    block_len = math.gcd(total_cells, 1024)
    block_count = total_cells // block_len
    analysis = ensemble.reshape(members, total_cells)

    def own_prior(field, batch_id):
        cell_ids = lax.dynamic_slice(obs_cell, (batch_id, device * OBS_DEV), (1, OBS_DEV))[0]
        return (jnp.take(field, cell_ids, axis=1), cell_ids)

    def collect(prior_now):
        panel_now = lax.all_gather(prior_now, ("gx", "gy"), axis=1, tiled=True)
        obs_index = jnp.arange(panel_now.shape[1], dtype=jnp.int32)
        return (panel_now, obs_index)

    prior_now, unused = own_prior(analysis, 0)
    panel_now, obs_index = collect(prior_now)
    for batch_id in range(BATCHES):
        prepare_cell_ids = jnp.take(obs_cell[batch_id], obs_index)
        prepare_obs_x, prepare_obs_y = locate(obs_index, prepare_cell_ids, gy_count)
        prepare_packed = statistics(
            panel_now,
            jnp.take(obs_error[batch_id], obs_index),
            jnp.take(obs_values[batch_id], obs_index),
        )
        prepare_radius = band_offsets[batch_id].astype(jnp.float32)
        obs_x = prepare_obs_x
        obs_y = prepare_obs_y
        radius = prepare_radius
        packed = prepare_packed
        if batch_id + 1 < BATCHES:
            next_id = batch_id + 1

        def sweep(block_id, field):
            start = block_id * block_len
            columns = lax.dynamic_slice_in_dim(field, start, block_len, 1)
            local_ids = start + jnp.arange(block_len, dtype=jnp.int32)
            cell_x = gx_pos * CX + local_ids // row_len
            cell_y = gy_pos * CY + local_ids % row_len // LEVELS
            fresh = update_cells(columns, cell_x, cell_y, obs_x, obs_y, radius, extent, packed)
            return lax.dynamic_update_slice_in_dim(field, fresh, start, 1)

        analysis = lax.fori_loop(0, block_count, sweep, analysis)
        if batch_id + 1 < BATCHES:
            prior_next, unused = own_prior(analysis, next_id)
            upcoming = collect(prior_next)
            panel_now, obs_index = upcoming
    return analysis.reshape(ensemble.shape)


def solution(mesh):
    in_specs = (P(None, "gx", "gy"), P(), P(), P(), P())
    out_specs = P(None, "gx", "gy")
    return jax.shard_map(
        per_device, mesh=mesh, in_specs=in_specs, out_specs=out_specs, check_vma=False
    )
```

profile of v0, /device:TPU:0, one launch (start us, length us, event | category | flops | bytes accessed | tf_op | source)
XLA Modules:
  0.0 312.3 jit_solution(8381231549604133119)
XLA Ops:
  3.0 4.5 %gather_fusion = s32[1024]{0:T(1024)S(1)} fusion(s32[1024]{0:T(1024)S(1)} %bitcast.84, s32[1024]{0:T(1024)S(1)} %iota_clamp_fusion), kind=kCustom, calls=%fused_computation.1.clone | custom fusion | bytes 12288 | tf_op jit(solution)/shard_map/jit(_take)/gather | solution.py:89
  10.2 72.5 %all_gather.9 = f32[80,1024]{0,1:T(8,128)S(1)} all-gather(f32[80,32]{0,1:T(8,128)S(1)} %select_bitcast_fusion.2), channel_id=1, replica_groups=mesh['gx'=8,'gy'=4] {'gx','gy'}, dimensions={1}, use_global_device_ids=true | all-gather | bytes 337920 | tf_op jit(solution)/shard_map/all_gather | solution.py:82
  83.3 4.5 %gather_fusion.3 = f32[1024]{0:T(1024)S(1)} fusion(f32[1024]{0:T(1024)S(1)} %bitcast.85, s32[1024]{0:T(1024)S(1)} %iota_clamp_fusion), kind=kCustom, calls=%fused_computation.7.clone | custom fusion | bytes 12288 | tf_op jit(solution)/shard_map/jit(_take)/gather | solution.py:94
  89.0 4.5 %gather_fusion.2 = f32[1024]{0:T(1024)S(1)} fusion(f32[1024]{0:T(1024)S(1)} %bitcast.86, s32[1024]{0:T(1024)S(1)} %iota_clamp_fusion), kind=kCustom, calls=%fused_computation.2.clone | custom fusion | bytes 12288 | tf_op jit(solution)/shard_map/jit(_take)/gather | solution.py:93
  94.6 15.5 %while.48 = (s32[]{:T(128)}, f32[80,3072]{1,0:T(8,128)S(1)}, s32[]{:T(128)}, s32[1024]{0:T(1024)S(1)}, f32[]{:T(128)}, /*index=5*/s32[]{:T(128)}, s32[1024]{0:T(...) while((s32[]{:T(128)}, f32[80,3072]{1,0:T(8,128)S(1)}, ...), condition=%wide.region_4.8_spmd, body=%wide.region_2.7_spmd.sunk | while | flops 367532032 | bytes 2379991 | solution.py:113
  94.7 5.0 %fusion.137 = f32[81,1024]{1,0:T(8,128)S(1)} fusion(bf16[81,1024]{1,0:T(8,128)(2,1)S(1)} %get-tuple-element.1279, bf16[80,1024]{1,0:T(8,128)(2,1)S(1)} %get-tuple-element.1277, f32[1024]{0:T(1024)S(1)} %get-tuple-element.1278, s32[1024]{0:T(1024)S(1)} %get-tuple-element.1276, s32[1024]{0:T(1024)S(1)} %get-tuple-element.1216, ...), kind=kOutput, calls=%fused_computation.18.clone.1 | convolution fusion | flops 367165440 | bytes 1028104 | tf_op jit(solution)/shard_map/while/body/eval_jaxpr/dot_general | solution.py:58
  99.9 5.0 %fusion.137 = f32[81,1024]{1,0:T(8,128)S(1)} fusion(bf16[81,1024]{1,0:T(8,128)(2,1)S(1)} %get-tuple-element.1279, bf16[80,1024]{1,0:T(8,128)(2,1)S(1)} %get-tuple-element.1277, f32[1024]{0:T(1024)S(1)} %get-tuple-element.1278, s32[1024]{0:T(1024)S(1)} %get-tuple-element.1276, s32[1024]{0:T(1024)S(1)} %get-tuple-element.1216, ...), kind=kOutput, calls=%fused_computation.18.clone.1 | convolution fusion | flops 367165440 | bytes 1028104 | tf_op jit(solution)/shard_map/while/body/eval_jaxpr/dot_general | solution.py:58
  105.0 5.0 %fusion.137 = f32[81,1024]{1,0:T(8,128)S(1)} fusion(bf16[81,1024]{1,0:T(8,128)(2,1)S(1)} %get-tuple-element.1279, bf16[80,1024]{1,0:T(8,128)(2,1)S(1)} %get-tuple-element.1277, f32[1024]{0:T(1024)S(1)} %get-tuple-element.1278, s32[1024]{0:T(1024)S(1)} %get-tuple-element.1276, s32[1024]{0:T(1024)S(1)} %get-tuple-element.1216, ...), kind=kOutput, calls=%fused_computation.18.clone.1 | convolution fusion | flops 367165440 | bytes 1028104 | tf_op jit(solution)/shard_map/while/body/eval_jaxpr/dot_general | solution.py:58
  110.1 4.5 %gather_fusion.4 = s32[1024]{0:T(1024)S(1)} fusion(s32[1024]{0:T(1024)S(1)} %bitcast.81, s32[1024]{0:T(1024)S(1)} %iota_clamp_fusion), kind=kCustom, calls=%fused_computation.5.clone | custom fusion | bytes 12288 | tf_op jit(solution)/shard_map/jit(_take)/gather | solution.py:89
  116.5 66.3 %all_gather.10 = f32[80,1024]{0,1:T(8,128)S(1)} all-gather(f32[80,32]{0,1:T(8,128)S(1)} %select_bitcast_fusion.1), channel_id=1, replica_groups=mesh['gx'=8,'gy'=4] {'gx','gy'}, dimensions={1}, use_global_device_ids=true | all-gather | bytes 337920 | tf_op jit(solution)/shard_map/all_gather | solution.py:82
  182.7 4.5 %gather_fusion.7 = f32[1024]{0:T(1024)S(1)} fusion(f32[1024]{0:T(1024)S(1)} %bitcast.82, s32[1024]{0:T(1024)S(1)} %iota_clamp_fusion), kind=kCustom, calls=%fused_computation.9.clone | custom fusion | bytes 12288 | tf_op jit(solution)/shard_map/jit(_take)/gather | solution.py:94
  187.9 4.5 %gather_fusion.6 = f32[1024]{0:T(1024)S(1)} fusion(f32[1024]{0:T(1024)S(1)} %bitcast.83, s32[1024]{0:T(1024)S(1)} %iota_clamp_fusion), kind=kCustom, calls=%fused_computation.8.clone | custom fusion | bytes 12288 | tf_op jit(solution)/shard_map/jit(_take)/gather | solution.py:93
  193.4 15.5 %while.49 = (s32[]{:T(128)}, f32[80,3072]{1,0:T(8,128)S(1)}, s32[]{:T(128)}, s32[1024]{0:T(1024)S(1)}, f32[]{:T(128)}, /*index=5*/s32[]{:T(128)}, s32[1024]{0:T(...) while((s32[]{:T(128)}, f32[80,3072]{1,0:T(8,128)S(1)}, ...), condition=%wide.region_9.13_spmd, body=%wide.region_7.12_spmd.sunk | while | flops 367532032 | bytes 2379991 | solution.py:113
  193.5 5.0 %fusion.142 = f32[81,1024]{1,0:T(8,128)S(1)} fusion(bf16[81,1024]{1,0:T(8,128)(2,1)S(1)} %get-tuple-element.1321, bf16[80,1024]{1,0:T(8,128)(2,1)S(1)} %get-tuple-element.1319, f32[1024]{0:T(1024)S(1)} %get-tuple-element.1320, s32[1024]{0:T(1024)S(1)} %get-tuple-element.1318, s32[1024]{0:T(1024)S(1)} %get-tuple-element.1228, ...), kind=kOutput, calls=%fused_computation.58.clone.1 | convolution fusion | flops 367165440 | bytes 1028104 | tf_op jit(solution)/shard_map/while/body/eval_jaxpr/dot_general | solution.py:58
  198.7 5.0 %fusion.142 = f32[81,1024]{1,0:T(8,128)S(1)} fusion(bf16[81,1024]{1,0:T(8,128)(2,1)S(1)} %get-tuple-element.1321, bf16[80,1024]{1,0:T(8,128)(2,1)S(1)} %get-tuple-element.1319, f32[1024]{0:T(1024)S(1)} %get-tuple-element.1320, s32[1024]{0:T(1024)S(1)} %get-tuple-element.1318, s32[1024]{0:T(1024)S(1)} %get-tuple-element.1228, ...), kind=kOutput, calls=%fused_computation.58.clone.1 | convolution fusion | flops 367165440 | bytes 1028104 | tf_op jit(solution)/shard_map/while/body/eval_jaxpr/dot_general | solution.py:58
  203.9 5.0 %fusion.142 = f32[81,1024]{1,0:T(8,128)S(1)} fusion(bf16[81,1024]{1,0:T(8,128)(2,1)S(1)} %get-tuple-element.1321, bf16[80,1024]{1,0:T(8,128)(2,1)S(1)} %get-tuple-element.1319, f32[1024]{0:T(1024)S(1)} %get-tuple-element.1320, s32[1024]{0:T(1024)S(1)} %get-tuple-element.1318, s32[1024]{0:T(1024)S(1)} %get-tuple-element.1228, ...), kind=kOutput, calls=%fused_computation.58.clone.1 | convolution fusion | flops 367165440 | bytes 1028104 | tf_op jit(solution)/shard_map/while/body/eval_jaxpr/dot_general | solution.py:58
  209.6 4.5 %gather_fusion.8 = s32[1024]{0:T(1024)S(1)} fusion(s32[1024]{0:T(1024)S(1)} %bitcast.78, s32[1024]{0:T(1024)S(1)} %iota_clamp_fusion), kind=kCustom, calls=%fused_computation.6.clone | custom fusion | bytes 12288 | tf_op jit(solution)/shard_map/jit(_take)/gather | solution.py:89
  216.0 68.9 %all_gather.11 = f32[80,1024]{0,1:T(8,128)S(1)} all-gather(f32[80,32]{0,1:T(8,128)S(1)} %select_bitcast_fusion), channel_id=1, replica_groups=mesh['gx'=8,'gy'=4] {'gx','gy'}, dimensions={1}, use_global_device_ids=true | all-gather | bytes 337920 | tf_op jit(solution)/shard_map/all_gather | solution.py:82
  284.9 4.5 %gather_fusion.11 = f32[1024]{0:T(1024)S(1)} fusion(f32[1024]{0:T(1024)S(1)} %bitcast.79, s32[1024]{0:T(1024)S(1)} %iota_clamp_fusion), kind=kCustom, calls=%fused_computation.11.clone | custom fusion | bytes 12288 | tf_op jit(solution)/shard_map/jit(_take)/gather | solution.py:94
  290.1 4.5 %gather_fusion.10 = f32[1024]{0:T(1024)S(1)} fusion(f32[1024]{0:T(1024)S(1)} %bitcast.80, s32[1024]{0:T(1024)S(1)} %iota_clamp_fusion), kind=kCustom, calls=%fused_computation.10.clone | custom fusion | bytes 12288 | tf_op jit(solution)/shard_map/jit(_take)/gather | solution.py:93
  295.7 15.5 %while.50 = (s32[]{:T(128)}, f32[80,3072]{1,0:T(8,128)S(1)}, s32[]{:T(128)}, s32[1024]{0:T(1024)S(1)}, f32[]{:T(128)}, /*index=5*/s32[]{:T(128)}, s32[1024]{0:T(...) while((s32[]{:T(128)}, f32[80,3072]{1,0:T(8,128)S(1)}, ...), condition=%wide.region_14.18_spmd, body=%wide.region_12.17_spmd.sunk | while | flops 367532032 | bytes 2379991 | solution.py:113
  295.8 5.0 %fusion.147 = f32[81,1024]{1,0:T(8,128)S(1)} fusion(bf16[81,1024]{1,0:T(8,128)(2,1)S(1)} %get-tuple-element.1363, bf16[80,1024]{1,0:T(8,128)(2,1)S(1)} %get-tuple-element.1361, f32[1024]{0:T(1024)S(1)} %get-tuple-element.1362, s32[1024]{0:T(1024)S(1)} %get-tuple-element.1360, s32[1024]{0:T(1024)S(1)} %get-tuple-element.1240, ...), kind=kOutput, calls=%fused_computation.98.clone.1 | convolution fusion | flops 367165440 | bytes 1028104 | tf_op jit(solution)/shard_map/while/body/eval_jaxpr/dot_general | solution.py:58
  300.9 5.0 %fusion.147 = f32[81,1024]{1,0:T(8,128)S(1)} fusion(bf16[81,1024]{1,0:T(8,128)(2,1)S(1)} %get-tuple-element.1363, bf16[80,1024]{1,0:T(8,128)(2,1)S(1)} %get-tuple-element.1361, f32[1024]{0:T(1024)S(1)} %get-tuple-element.1362, s32[1024]{0:T(1024)S(1)} %get-tuple-element.1360, s32[1024]{0:T(1024)S(1)} %get-tuple-element.1240, ...), kind=kOutput, calls=%fused_computation.98.clone.1 | convolution fusion | flops 367165440 | bytes 1028104 | tf_op jit(solution)/shard_map/while/body/eval_jaxpr/dot_general | solution.py:58
  306.1 5.0 %fusion.147 = f32[81,1024]{1,0:T(8,128)S(1)} fusion(bf16[81,1024]{1,0:T(8,128)(2,1)S(1)} %get-tuple-element.1363, bf16[80,1024]{1,0:T(8,128)(2,1)S(1)} %get-tuple-element.1361, f32[1024]{0:T(1024)S(1)} %get-tuple-element.1362, s32[1024]{0:T(1024)S(1)} %get-tuple-element.1360, s32[1024]{0:T(1024)S(1)} %get-tuple-element.1240, ...), kind=kOutput, calls=%fused_computation.98.clone.1 | convolution fusion | flops 367165440 | bytes 1028104 | tf_op jit(solution)/shard_map/while/body/eval_jaxpr/dot_general | solution.py:58
  (113 shorter events, 16.3 us)
Async XLA Ops:
  1.7 0.7 copy-start.3
  3.0 4.6 %copy-start.6 = (s32[3]{0:T(128)S(1)}, s32[3]{0:T(128)}, u32[]{:S(2)}) copy-start(s32[3]{0:T(128)} %param.21) | copy-start | bytes 40
  3.0 79.7 %copy-start.4 = (f32[3,1024]{1,0:T(4,128)S(1)}, f32[3,1024]{1,0:T(4,128)}, u32[]{:S(2)}) copy-start(f32[3,1024]{1,0:T(4,128)} %param.18) | copy-start | bytes 36868
  83.3 5.1 %copy-start.5 = (f32[3,1024]{1,0:T(4,128)S(1)}, f32[3,1024]{1,0:T(4,128)}, u32[]{:S(2)}) copy-start(f32[3,1024]{1,0:T(4,128)} %param.19) | copy-start | bytes 36868
  209.0 0.7 copy-start
  214.2 1.2 copy-start.8
  214.2 1.8 copy-start.7
  214.9 70.1 %copy-start.1 = (f32[1,1024]{1,0:T(1,128)S(1)}, f32[1,1024]{1,0:T(1,128)}, u32[]{:S(2)}) copy-start(f32[1,1024]{1,0:T(1,128)} %get-tuple-element.1013) | copy-start | bytes 12292
  289.4 0.7 copy-start.2
where the time goes:
time: 313 us; the launch traced here: 312 us
  blocking collectives  208 us (66%)
  local copies, waits for them, and re-layouts  51.6 us (16%)
  matrix products  44.8 us (14%)
  other arithmetic  5.49 us (2%)
    all_gather x3, blocking collectives, collect(): panel_now = lax.all_gather(prior_now, ('gx', 'gy'), axis=1, tiled=True)  208 us
    dot_general x9, matrix products, update_cells(): lax.dot_general(weighted, gain_wts, (((1,), (1,)), ((), ())), preferred_e...  44.8 us
    gather x3, local copies, waits for them, and re-layouts, per_device(): prepare_cell_ids = jnp.take(obs_cell[batch_id], obs_index)  13.6 us
    gather x3, local copies, waits for them, and re-layouts, per_device(): jnp.take(obs_error[batch_id], obs_index)  13.6 us
    gather x3, local copies, waits for them, and re-layouts, per_device(): jnp.take(obs_values[batch_id], obs_index)  13.6 us

commit v1 on v0

v1 whole, which is shorter than its diff:
```python
import functools

import jax
import jax.numpy as jnp
from jax import lax
from jax.experimental import pallas as pl
from jax.experimental.pallas import tpu as pltpu
from jax.sharding import PartitionSpec as P

LEVELS = 8
CY = 16
CX = 24
OBS_DEV = 32
LANES = 128
MEAN, XPOS, YPOS, ERR, VAL = 80, 81, 82, 83, 84
BLOCK_OBS = 256


def pick_kernel(gx_count, gy_count, members, batches, pos, cell, error, value, x_ref, z_ref, g_ref):
    cells_x, column = CX, CY * LEVELS
    sub = lax.broadcasted_iota(jnp.int32, (8, column), 0)
    for x in range(cells_x):
        block = x_ref[pl.ds(x, members, stride=cells_x), :]
        mean = jnp.sum(block, axis=0, keepdims=True) * (1.0 / members)
        mean_rows = jnp.where(sub == 0, mean, 0.0)
        rest = jnp.zeros((LANES - members - 8, column), jnp.float32)
        full = jnp.concatenate([block - mean, mean_rows, rest], axis=0)
        z_ref[x * column : (x + 1) * column, :] = full.T
    lane = lax.broadcasted_iota(jnp.int32, (1, LANES), 1)
    first = (pos[0] * gy_count + pos[1]) * OBS_DEV
    for b in range(batches):
        for r in range(OBS_DEV):
            c = cell[b, first + r]
            row = z_ref[pl.ds(c, 1), :]
            ox = (pos[0] * CX + c // column).astype(jnp.float32)
            oy = (pos[1] * CY + c % column // LEVELS).astype(jnp.float32)
            row = jnp.where(lane == XPOS, ox, row)
            row = jnp.where(lane == YPOS, oy, row)
            row = jnp.where(lane == ERR, error[b, first + r], row)
            row = jnp.where(lane == VAL, value[b, first + r], row)
            g_ref[b * OBS_DEV + r : b * OBS_DEV + r + 1, :] = row


def taper(distance, inverse):
    left = jnp.maximum(1.0 - distance * inverse, 0.0)
    return left * left * (3.0 - 2.0 * left)


def sweep_kernel(gx_count, gy_count, members, batches, masks, pos, radius, *refs):
    gathered, (z_in, out_ref, z, cells, rows, obs_cells, hp, rhs, line) = refs[:-9], refs[-9:]
    column = CY * LEVELS
    own_rows = batches * OBS_DEV
    group = gy_count * OBS_DEV
    per_block = max(1, BLOCK_OBS // group)
    block = per_block * group
    obs = gx_count * group
    extent = float(gx_count * CX)
    gx, gy = pos[0], pos[1]

    here = 0
    for part in gathered:
        for i in range(part.shape[0] // own_rows):
            mx, my = masks[here]
            here += 1
            owner = (gx ^ mx) * gy_count + (gy ^ my)
            for b in range(batches):
                rows[b, pl.ds(pl.multiple_of(owner * OBS_DEV, OBS_DEV), OBS_DEV), :] = part[
                    i * own_rows + b * OBS_DEV : i * own_rows + (b + 1) * OBS_DEV, :
                ]

    sub16 = lax.broadcasted_iota(jnp.int32, (16, LANES), 0)
    sub8 = lax.broadcasted_iota(jnp.int32, (8, LANES), 0)
    latitude = (lax.broadcasted_iota(jnp.int32, (column, block), 0) // LEVELS).astype(jnp.float32)

    def prepare(b, start, slot, shift):
        t = rows[b, pl.ds(start, LANES), :].T
        pert = t[:members]
        var = jnp.sum(pert * pert, axis=0, keepdims=True) * (1.0 / (members - 1))
        err = t[ERR : ERR + 1]
        total = var + err
        scale = 1.0 / ((members - 1) * total)
        shrink = 1.0 / (1.0 + jnp.sqrt(err / total))
        innovation = t[VAL : VAL + 1] - t[MEAN : MEAN + 1]
        zeros = jnp.zeros((LANES - members - 16, LANES), jnp.bfloat16)
        pad = jnp.zeros((16, LANES), jnp.bfloat16)
        hp[:, pl.ds(slot, LANES)] = jnp.concatenate([pert.astype(jnp.bfloat16), pad, zeros], axis=0)
        tail = jnp.where(sub16 == 0, -innovation, 0.0).astype(jnp.bfloat16)
        rhs[:, pl.ds(slot, LANES)] = jnp.concatenate(
            [(shrink * pert).astype(jnp.bfloat16), tail, zeros], axis=0
        )
        ox = t[XPOS : XPOS + 1] + shift
        oy = t[YPOS : YPOS + 1]
        line[:, pl.ds(slot, LANES)] = jnp.where(
            sub8 == 0, ox, jnp.where(sub8 == 1, oy, jnp.where(sub8 == 2, scale, 0.0))
        )

    def window(first, count, body):
        def step(i, carry):
            at = first + i * per_block
            low, high = at < 0, at >= gx_count
            shift = jnp.where(low, extent, jnp.where(high, -extent, 0.0))
            at = at + jnp.where(low, gx_count, jnp.where(high, -gx_count, 0))
            lanes = pl.ds(pl.multiple_of(at * group, LANES), block)
            body(hp[:, lanes], rhs[:, lanes], line[0:1, lanes], line[1:2, lanes], line[2:3, lanes], shift)
            return carry

        lax.fori_loop(0, count, step, 0)

    def increment(cell_rows, pert, weight, right):
        cov = jnp.dot(cell_rows, pert, preferred_element_type=jnp.float32)
        gain = (cov * weight).astype(jnp.bfloat16)
        return lax.dot_general(
            gain, right, (((1,), (1,)), ((), ())), preferred_element_type=jnp.float32
        )

    z[...] = z_in[...]
    for b in range(batches):
        reach = (radius[b] - 2) // CX + 1
        inverse = 1.0 / jnp.full((1, 1), radius[b], jnp.int32).astype(jnp.float32)
        for g in range(obs // LANES):
            prepare(b, g * LANES, g * LANES, 0.0)
        for g in range((per_block - 1) * group // LANES):
            prepare(b, g * LANES, obs + g * LANES, extent)
        cells[...] = z[...].astype(jnp.bfloat16)

        def local(pert, right, ox, oy, scale, shift):
            by_row = taper(jnp.abs(latitude + (gy * CY).astype(jnp.float32) - oy), inverse) * scale
            for x in range(CX):
                here_x = (gx * CX + x).astype(jnp.float32) + shift
                weight = taper(jnp.abs(here_x - ox), inverse) * by_row
                at = slice(x * column, (x + 1) * column)
                z[at, :] = z[at, :] - increment(cells[at, :], pert, weight, right)

        window(gx - reach, (2 * reach + per_block) // per_block, local)

        later = range(b + 1, batches)
        for nb in later:
            obs_cells[nb] = rows[nb].astype(jnp.bfloat16)

        def one_group(q, carry):
            def remote(pert, right, ox, oy, scale, shift):
                for nb in later:
                    at = pl.ds(pl.multiple_of(q * block, block), block)
                    state = rows[nb, at, :]
                    by_x = taper(jnp.abs(state[:, XPOS : XPOS + 1] + shift - ox), inverse)
                    by_y = taper(jnp.abs(state[:, YPOS : YPOS + 1] - oy), inverse)
                    rows[nb, at, :] = state - increment(
                        obs_cells[nb, at, :], pert, by_x * by_y * scale, right
                    )

            window(q * per_block - reach, (2 * reach + 2 * per_block - 1) // per_block, remote)
            return carry

        if b + 1 < batches:
            lax.fori_loop(0, obs // block, one_group, 0)

    for x in range(CX):
        t = z[x * column : (x + 1) * column, :].T
        out_ref[pl.ds(x, members, stride=CX), :] = t[:members] + t[MEAN : MEAN + 1]


def exchange(rows, gx_count, gy_count):
    gx_bits = [1 << i for i in range(gx_count.bit_length() - 1)]
    gy_bits = [1 << i for i in range(gy_count.bit_length() - 1)]
    steps = [("gx", bit) for bit in reversed(gx_bits[1:])]
    steps += [("gy", bit) for bit in reversed(gy_bits)] + [("gx", bit) for bit in gx_bits[:1]]
    masks = [(0, 0)]
    parts = [rows]
    for axis, bit in steps:
        held = parts[0] if len(parts) == 1 else jnp.concatenate(parts, axis=0)
        size = gx_count if axis == "gx" else gy_count
        other = lax.ppermute(held, axis, [(i, i ^ bit) for i in range(size)])
        parts = [held, other]
        move = (bit, 0) if axis == "gx" else (0, bit)
        masks = masks + [(mx ^ move[0], my ^ move[1]) for mx, my in masks]
    return parts, masks


def per_device(gx_count, gy_count, ensemble, obs_values, obs_error, obs_cell, band_offsets):
    members, rows_here, row_len = ensemble.shape
    batches, obs = obs_cell.shape
    total = rows_here * row_len
    group = gy_count * OBS_DEV
    per_block = max(1, BLOCK_OBS // group)
    padded = obs + (per_block - 1) * group
    pos = jnp.stack([lax.axis_index("gx"), lax.axis_index("gy")]).astype(jnp.int32)
    smem = pl.BlockSpec(memory_space=pltpu.SMEM)
    vmem = pl.BlockSpec(memory_space=pltpu.VMEM)
    flat = ensemble.reshape(members * rows_here, row_len)
    z, own = pl.pallas_call(
        functools.partial(pick_kernel, gx_count, gy_count, members, batches),
        out_shape=(
            jax.ShapeDtypeStruct((total, LANES), jnp.float32),
            jax.ShapeDtypeStruct((batches * OBS_DEV, LANES), jnp.float32),
        ),
        in_specs=[smem, smem, smem, smem, vmem],
        out_specs=(vmem, vmem),
        name="pick",
    )(pos, obs_cell, obs_error, obs_values, flat)
    parts, masks = exchange(own, gx_count, gy_count)
    out = pl.pallas_call(
        functools.partial(sweep_kernel, gx_count, gy_count, members, batches, masks),
        out_shape=jax.ShapeDtypeStruct((members * rows_here, row_len), jnp.float32),
        in_specs=[smem, smem] + [vmem] * (len(parts) + 1),
        out_specs=vmem,
        scratch_shapes=[
            pltpu.VMEM((total, LANES), jnp.float32),
            pltpu.VMEM((total, LANES), jnp.bfloat16),
            pltpu.VMEM((batches, obs, LANES), jnp.float32),
            pltpu.VMEM((batches, obs, LANES), jnp.bfloat16),
            pltpu.VMEM((LANES, padded), jnp.bfloat16),
            pltpu.VMEM((LANES, padded), jnp.bfloat16),
            pltpu.VMEM((8, padded), jnp.float32),
        ],
        name="sweep",
    )(pos, band_offsets, *parts, z)
    return out.reshape(ensemble.shape)


def solution(mesh):
    in_specs = (P(None, "gx", "gy"), P(), P(), P(), P())
    out_specs = P(None, "gx", "gy")
    body = functools.partial(per_device, mesh.shape["gx"], mesh.shape["gy"])
    return jax.shard_map(
        body, mesh=mesh, in_specs=in_specs, out_specs=out_specs, check_vma=False
    )
```

time: 313 us -> 60.5 us (0.19)
  blocking collectives: 208 us -> 0 us
  local copies, waits for them, and re-layouts: 51.6 us -> 1.74 us
  matrix products: 44.8 us -> 0 us
  Pallas kernels: 0 us -> 30.2 us
  waiting for transfers between devices: 0 us -> 17.5 us
  starting transfers between devices: 0 us -> 9.05 us
    all_gather x3 -> x0, blocking collectives: 208 us -> none  [collect(): panel_now = lax.all_gather(prior_now, ('gx', 'gy'), axis=1, tiled=True)]
    dot_general x9 -> x0, matrix products: 44.8 us -> none  [update_cells(): lax.dot_general(weighted, gain_wts, (((1,), (1,)), ((), ())), preferred_e...]
    gather x12 -> x0, local copies, waits for them, and re-layouts: 42.4 us -> none  [the longest x3 13.6 us: per_device(): prepare_cell_ids = jnp.take(obs_cell[batch_id], obs_index)]
    pallas_call x0 -> x2, Pallas kernels: none -> 30.2 us  [the longest x1 26.4 us: per_device(): pl.pallas_call(functools.partial(sweep_kernel, gx_count, gy_count, member...]
    ppermute x0 -> x5, waiting for transfers between devices: none -> 17.5 us  [exchange(): other = lax.ppermute(held, axis, [(i, i ^ bit) for i in range(size)])]
    ppermute x0 -> x5, starting transfers between devices: none -> 9.05 us  [exchange(): other = lax.ppermute(held, axis, [(i, i ^ bit) for i in range(size)])]
  transfers between devices with their start and end apart: 0 -> 5, of which waited for: 0 -> 5; matrix products, arithmetic and copies ran while one was open for 0% -> 1% of each run, Pallas kernels for 0% -> 0%
where the time goes in v1:
time: 60.5 us; the launch traced here: 61.5 us
  Pallas kernels  30.2 us (50%)
  waiting for transfers between devices  17.5 us (29%)
  starting transfers between devices  9.05 us (15%)
  other arithmetic  3.03 us (5%)
  local copies, waits for them, and re-layouts  1.74 us (3%)
    pallas_call x1, Pallas kernels, per_device(): pl.pallas_call(functools.partial(sweep_kernel, gx_count, gy_count, member...  26.4 us
    ppermute x5, waiting for transfers between devices, exchange(): other = lax.ppermute(held, axis, [(i, i ^ bit) for i in range(size)])  17.5 us
    ppermute x5, starting transfers between devices, exchange(): other = lax.ppermute(held, axis, [(i, i ^ bit) for i in range(size)])  9.05 us
    pallas_call x1, Pallas kernels, per_device(): pl.pallas_call(functools.partial(pick_kernel, gx_count, gy_count, members...  3.74 us
    concatenate x3, other arithmetic, exchange(): held = parts[0] if len(parts) == 1 else jnp.concatenate(parts, axis=0)  2.44 us
    unnamed x8, local copies, waits for them, and re-layouts  1.72 us
  transfers between devices with their start and end apart: 5, of which 5 were waited for; matrix products, arithmetic and copies ran while one was open for 1% of the time, Pallas kernels for 0%

profile of v1, /device:TPU:0, one launch (start us, length us, event | category | flops | bytes accessed | tf_op | source)
XLA Modules:
  0.0 61.5 jit_solution(13831144796437273551)
XLA Ops:
  0.0 0.6 pad_add_fusion.pos
  0.6 3.7 %pick.1 = (f32[3072,128]{1,0:T(8,128)}, f32[96,128]{1,0:T(8,128)}) custom-call(s32[2]{0:T(128)} %pad_add_fusion.pos, s32[3,1024]{1,0:T(4,128)} %cell.1, f32[3,1024]{1,0:T(4,128)} %error.1, f32[3,1024]{1,0:T(4,128)} %value.1, f32[1920,128]{1,0:T(8,128)} %bitcast.4), custom_call_target="tpu_custom_call" | custom-call | tf_op jit(solution)/shard_map/pick/pallas_call | solution.py:190
  4.3 4.0 %collective-permute-start = (f32[96,128]{1,0:T(8,128)}, f32[96,128]{1,0:T(8,128)S(1)}, u32[]{:S(2)}, u32[]{:S(2)}) collective-permute-start(f32[96,128]{1,0:T(8,128)} %get-tuple-element.7), channel_id=1, source_target_pairs={{0,16},{4,20},{8,24},{12,28},{16,0},{20,4},{24,8},{28,12},{1,17},{... | collective-permute-start | bytes 147464 | tf_op jit(solution)/shard_map/ppermute | solution.py:172
  8.4 2.8 %collective-permute-done = f32[96,128]{1,0:T(8,128)S(1)} collective-permute-done((f32[96,128]{1,0:T(8,128)}, f32[96,128]{1,0:T(8,128)S(1)}, u32[]{:S(2)}, u32[]{:S(2)}) %collective-permute-start) | collective-permute-done | bytes 49184 | tf_op jit(solution)/shard_map/ppermute | solution.py:172
  11.2 0.8 %pad_maximum_fusion.2 = f32[192,128]{1,0:T(8,128)S(1)} fusion(f32[96,128]{1,0:T(8,128)S(1)} %collective-permute-done, f32[96,128]{1,0:T(8,128)} %get-tuple-element.7), kind=kLoop, calls=%fused_computation.2 | loop fusion | flops 24576 | bytes 196608 | tf_op jit(solution)/shard_map/concatenate | solution.py:170
  12.0 1.4 %collective-permute-start.1 = (f32[192,128]{1,0:T(8,128)S(1)}, f32[192,128]{1,0:T(8,128)S(1)}, u32[]{:S(2)}, u32[]{:S(2)}) collective-permute-start(f32[192,128]{1,0:T(8,128)S(1)} %pad_maximum_fusion.2), channel_id=1, source_target_pairs={{0,8},{4,12},{8,0},{12,4},{16,24},{20,28},{24,16},{28,20},{1,9},{5... | collective-permute-start | bytes 294920 | tf_op jit(solution)/shard_map/ppermute | solution.py:172
  13.4 3.2 %collective-permute-done.1 = f32[192,128]{1,0:T(8,128)S(1)} collective-permute-done((f32[192,128]{1,0:T(8,128)S(1)}, f32[192,128]{1,0:T(8,128)S(1)}, u32[]{:S(2)}, u32[]{:S(2)}) %collective-permute-start.1) | collective-permute-done | bytes 98336 | tf_op jit(solution)/shard_map/ppermute | solution.py:172
  16.6 0.8 %pad_maximum_fusion.1 = f32[384,128]{1,0:T(8,128)S(1)} fusion(f32[192,128]{1,0:T(8,128)S(1)} %collective-permute-done.1, f32[96,128]{1,0:T(8,128)S(1)} %collective-permute-done, f32[96,128]{1,0:T(8,128)} %get-tuple-element.7), kind=kLoop, calls=%fused_computation.1 | loop fusion | flops 98304 | bytes 393216 | tf_op jit(solution)/shard_map/concatenate | solution.py:170
  17.4 1.8 %collective-permute-start.2 = (f32[384,128]{1,0:T(8,128)S(1)}, f32[384,128]{1,0:T(8,128)S(1)}, u32[]{:S(2)}, u32[]{:S(2)}) collective-permute-start(f32[384,128]{1,0:T(8,128)S(1)} %pad_maximum_fusion.1), channel_id=1, source_target_pairs={{0,2},{1,3},{2,0},{3,1},{4,6},{5,7},{6,4},{7,5},{8,10},{9,11},{10,... | collective-permute-start | bytes 589832 | tf_op jit(solution)/shard_map/ppermute | solution.py:172
  19.2 3.9 %collective-permute-done.2 = f32[384,128]{1,0:T(8,128)S(1)} collective-permute-done((f32[384,128]{1,0:T(8,128)S(1)}, f32[384,128]{1,0:T(8,128)S(1)}, u32[]{:S(2)}, u32[]{:S(2)}) %collective-permute-start.2) | collective-permute-done | bytes 196640 | tf_op jit(solution)/shard_map/ppermute | solution.py:172
  23.1 0.8 %pad_maximum_fusion = f32[768,128]{1,0:T(8,128)S(1)} fusion(f32[384,128]{1,0:T(8,128)S(1)} %collective-permute-done.2, f32[192,128]{1,0:T(8,128)S(1)} %collective-permute-done.1, f32[96,128]{1,0:T(8,128)S(1)} %collective-permute-done, f32[96,128]{1,0:T(8,128)} %get-tuple-element.7), kind=kLoop, calls=%fused_computation | loop fusion | flops 294912 | bytes 786432 | tf_op jit(solution)/shard_map/concatenate | solution.py:170
  24.0 1.8 %collective-permute-start.3 = (f32[768,128]{1,0:T(8,128)S(1)}, f32[768,128]{1,0:T(8,128)S(1)}, u32[]{:S(2)}, u32[]{:S(2)}) collective-permute-start(f32[768,128]{1,0:T(8,128)S(1)} %pad_maximum_fusion), channel_id=1, source_target_pairs={{0,1},{1,0},{2,3},{3,2},{4,5},{5,4},{6,7},{7,6},{8,9},{9,8},{10,11... | collective-permute-start | bytes 1179656 | tf_op jit(solution)/shard_map/ppermute | solution.py:172
  25.7 0.8 %constant_dynamic-update-slice_fusion.4 = f32[1536,128]{1,0:T(8,128)S(1)} fusion(f32[96,128]{1,0:T(8,128)} %get-tuple-element.7), kind=kLoop, calls=%fused_computation.7 | loop fusion | bytes 98304
  26.6 5.2 %collective-permute-done.3 = f32[768,128]{1,0:T(8,128)S(1)} collective-permute-done((f32[768,128]{1,0:T(8,128)S(1)}, f32[768,128]{1,0:T(8,128)S(1)}, u32[]{:S(2)}, u32[]{:S(2)}) %collective-permute-start.3) | collective-permute-done | bytes 393248 | tf_op jit(solution)/shard_map/ppermute | solution.py:172
  31.8 0.0 copy-start
  31.9 0.1 collective-permute-start.4
  31.9 2.3 %collective-permute-done.4.refs_1_ = f32[1536,128]{1,0:T(8,128)S(1)} collective-permute-done((f32[1536,128]{1,0:T(8,128)S(1)}, f32[1536,128]{1,0:T(8,128)S(1)}, u32[]{:S(2)}, u32[]{:S(2)}) %collective-permute-start.4) | collective-permute-done | bytes 786464 | tf_op jit(solution)/shard_map/ppermute | solution.py:172
  34.2 0.0 copy-start.1
  34.2 0.0 copy-done
  34.2 0.9 %copy-done.1 = f32[1536,128]{1,0:T(8,128)} copy-done((f32[1536,128]{1,0:T(8,128)}, f32[1536,128]{1,0:T(8,128)S(1)}, u32[]{:S(2)}) %copy-start.1) | copy-done | bytes 786456
  35.1 26.4 %sweep.1 = f32[1920,128]{1,0:T(8,128)} custom-call(s32[2]{0:T(128)} %pad_add_fusion.pos, s32[3]{0:T(128)} %radius.1, f32[1536,128]{1,0:T(8,128)} %copy-done, f32[1536,128]{1,0:T(8,128)} %copy-done.1, f32[3072,128]{1,0:T(8,128)} %get-tuple-element.8.refs_2_), custom_call_target="tpu_custom_call" | custom-call | tf_op jit(solution)/shard_map/sweep/pallas_call | solution.py:201
  (4 shorter events, 0.1 us)
Async XLA Ops:
  4.3 6.8 %collective-permute-start = (f32[96,128]{1,0:T(8,128)}, f32[96,128]{1,0:T(8,128)S(1)}, u32[]{:S(2)}, u32[]{:S(2)}) collective-permute-start(f32[96,128]{1,0:T(8,128)} %get-tuple-element.7), channel_id=1, source_target_pairs={{0,16},{4,20},{8,24},{12,28},{16,0},{20,4},{24,8},{28,12},{1,17},{... | collective-permute-start | bytes 147464 | tf_op jit(solution)/shard_map/ppermute | solution.py:172
  12.0 4.6 %collective-permute-start.1 = (f32[192,128]{1,0:T(8,128)S(1)}, f32[192,128]{1,0:T(8,128)S(1)}, u32[]{:S(2)}, u32[]{:S(2)}) collective-permute-start(f32[192,128]{1,0:T(8,128)S(1)} %pad_maximum_fusion.2), channel_id=1, source_target_pairs={{0,8},{4,12},{8,0},{12,4},{16,24},{20,28},{24,16},{28,20},{1,9},{5... | collective-permute-start | bytes 294920 | tf_op jit(solution)/shard_map/ppermute | solution.py:172
  17.4 5.7 %collective-permute-start.2 = (f32[384,128]{1,0:T(8,128)S(1)}, f32[384,128]{1,0:T(8,128)S(1)}, u32[]{:S(2)}, u32[]{:S(2)}) collective-permute-start(f32[384,128]{1,0:T(8,128)S(1)} %pad_maximum_fusion.1), channel_id=1, source_target_pairs={{0,2},{1,3},{2,0},{3,1},{4,6},{5,7},{6,4},{7,5},{8,10},{9,11},{10,... | collective-permute-start | bytes 589832 | tf_op jit(solution)/shard_map/ppermute | solution.py:172
  24.0 7.8 %collective-permute-start.3 = (f32[768,128]{1,0:T(8,128)S(1)}, f32[768,128]{1,0:T(8,128)S(1)}, u32[]{:S(2)}, u32[]{:S(2)}) collective-permute-start(f32[768,128]{1,0:T(8,128)S(1)} %pad_maximum_fusion), channel_id=1, source_target_pairs={{0,1},{1,0},{2,3},{3,2},{4,5},{5,4},{6,7},{7,6},{8,9},{9,8},{10,11... | collective-permute-start | bytes 1179656 | tf_op jit(solution)/shard_map/ppermute | solution.py:172
  31.8 2.4 %copy-start = (f32[1536,128]{1,0:T(8,128)}, f32[1536,128]{1,0:T(8,128)S(1)}, u32[]{:S(2)}) copy-start(f32[1536,128]{1,0:T(8,128)S(1)} %constant_dynamic-update-slice_fusion.refs_0_) | copy-start | bytes 2359300
  31.9 2.4 %collective-permute-start.4 = (f32[1536,128]{1,0:T(8,128)S(1)}, f32[1536,128]{1,0:T(8,128)S(1)}, u32[]{:S(2)}, u32[]{:S(2)}) collective-permute-start(f32[1536,128]{1,0:T(8,128)S(1)} %constant_dynamic-update-slice_fusion.refs_0_), channel_id=1, source_target_pairs={{0,4},{4,0},{8,12},{12,8},{16,20},{20,16},{24,28},{28,24},{1,5},{5... | collective-permute-start | bytes 2359304 | tf_op jit(solution)/shard_map/ppermute | solution.py:172
  34.2 0.9 %copy-start.1 = (f32[1536,128]{1,0:T(8,128)}, f32[1536,128]{1,0:T(8,128)S(1)}, u32[]{:S(2)}) copy-start(f32[1536,128]{1,0:T(8,128)S(1)} %collective-permute-done.4.refs_1_) | copy-start | bytes 2359300

commit v2 on v0

v2 whole, which is shorter than its diff:
```python
import functools

import jax
import jax.numpy as jnp
from jax import lax
from jax.experimental import pallas as pl
from jax.experimental.pallas import tpu as pltpu
from jax.sharding import PartitionSpec as P

LEVELS = 8
CY = 16
CX = 24
COLUMN = CY * LEVELS
OBS_DEV = 32
LANES = 128
MEAN, ERR = 80, 81
USED = 82
SPILL = LANES - USED
BLOCK_OBS = 256
PICK = 32
COLUMNS = 4
PIECES = 4
RADIUS_MAX = 71
STORED_MAX = 16 << 20
VMEM_LIMIT = 24 << 20
PICK_LIMIT = 60 << 20


class Layout:
    def __init__(self, gx_count, gy_count, batches):
        self.gx, self.gy, self.batches = gx_count, gy_count, batches
        self.group = gy_count * OBS_DEV
        self.per_block = max(1, BLOCK_OBS // self.group)
        self.block = self.per_block * self.group
        self.obs = gx_count * self.group
        self.padded = self.obs + (self.per_block - 1) * self.group
        self.pick_rows = self.per_block * PICK
        self.extent = float(gx_count * CX)
        self.blocks = self.obs // self.block
        self.windows = self.window_count((RADIUS_MAX - 2) // CX + 1)
        size = 2 * self.blocks * self.windows * self.block * self.block
        self.stored = size * sum(range(batches)) <= STORED_MAX

    def window_count(self, reach):
        return (2 * reach + 2 * self.per_block - 1) // self.per_block

    def place(self, at):
        low, high = at < 0, at >= self.gx
        shift = jnp.where(low, self.extent, jnp.where(high, -self.extent, 0.0))
        at = at + jnp.where(low, self.gx, jnp.where(high, -self.gx, 0))
        return pl.ds(pl.multiple_of(at * self.group, LANES), self.block), shift


def iota(shape, dim):
    return lax.broadcasted_iota(jnp.int32, shape, dim)


def dot(a, b):
    return jnp.dot(a, b, preferred_element_type=jnp.float32)


def taper(distance, inverse):
    left = jnp.maximum(1.0 - distance * inverse, 0.0)
    return left * left * (3.0 - 2.0 * left)


def inverse_of(radius):
    return 1.0 / jnp.full((1, 1), radius, jnp.int32).astype(jnp.float32)


def reach_of(radius):
    return (radius - 2) // CX + 1


def place_of(cell, start, lay):
    index = iota(cell.shape, 1) + start
    owner = index // OBS_DEV
    ox = owner // lay.gy * CX + cell // COLUMN
    oy = owner % lay.gy * CY + cell % COLUMN // LEVELS
    return ox.astype(jnp.float32), oy.astype(jnp.float32)


def turn_kernel(members, x_ref, z_ref):
    sub = iota((8, COLUMN), 0)
    for x in range(CX):
        block = x_ref[pl.ds(x, members, stride=CX), :]
        mean = jnp.sum(block, axis=0, keepdims=True) * (1.0 / members)
        rest = jnp.zeros((LANES - members - 8, COLUMN), jnp.float32)
        full = jnp.concatenate([block - mean, jnp.where(sub == 0, mean, 0.0), rest], axis=0)
        z_ref[x * COLUMN : (x + 1) * COLUMN, :] = full.T


def pick_kernel(lay, members, cell_in, error_in, value_in, x_in, own_ref, z_ref, x_ref, cell, error, value, rows, sems):
    small = [(cell_in, cell), (error_in, error), (value_in, value)]
    copies = [pltpu.make_async_copy(a, b, sems.at[i]) for i, (a, b) in enumerate(small)]
    part = x_ref.shape[0] // PIECES
    for i in range(PIECES):
        at = pl.ds(i * part, part)
        copies.append(pltpu.make_async_copy(x_in.at[at, :], x_ref.at[at, :], sems.at[len(small) + i]))
    for copy in copies:
        copy.start()
    for copy in copies:
        copy.wait()
    turn_kernel(members, x_ref, z_ref)
    first = (lax.axis_index("gx") * lay.gy + lax.axis_index("gy")) * OBS_DEV
    lane = iota((1, LANES), 1)
    for b in range(lay.batches):
        for r in range(OBS_DEV):
            row = z_ref[pl.ds(cell[b, first + r], 1), :]
            row = row - jnp.where(lane == MEAN, value[b, first + r], 0.0)
            row = jnp.where(lane == ERR, error[b, first + r], row)
            rows[b * OBS_DEV + r : b * OBS_DEV + r + 1, :] = row
    last = rows[2 * OBS_DEV : 3 * OBS_DEV, :]
    wide = iota((OBS_DEV, LANES), 1)
    own_ref[:OBS_DEV, :] = jnp.where(wide < USED, rows[:OBS_DEV, :], pltpu.roll(last, USED, 1))
    own_ref[OBS_DEV:, :] = jnp.where(wide < USED, rows[OBS_DEV : 2 * OBS_DEV, :], pltpu.roll(last, USED - SPILL, 1))


def fill_picks(lay, batch, cell, pick_x, pick_y, slot):
    diagonal = iota((LANES, LANES), 0) == iota((LANES, LANES), 1)
    lane_x = (iota((LANES, 2 * lay.pick_rows), 1) % lay.pick_rows).astype(jnp.float32)
    lane_y = (iota((LANES, 2 * lay.gy * CY), 1) % (lay.gy * CY)).astype(jnp.float32)
    for c in range(lay.obs // LANES):
        at = slice(c * LANES, (c + 1) * LANES)
        ox, oy = place_of(cell[batch : batch + 1, at], c * LANES, lay)
        g = c * LANES // lay.group
        ox = ox + float(g % lay.per_block * PICK - g * CX)
        both = jnp.sum(jnp.where(diagonal, ox * 1024.0 + oy, 0.0), axis=1, keepdims=True)
        down_x = jnp.floor(both * (1.0 / 1024.0))
        down_y = both - down_x * 1024.0
        pick_x[slot, at, :] = jnp.where(lane_x == down_x, 1.0, 0.0).astype(jnp.bfloat16)
        pick_y[slot, at, :] = jnp.where(lane_y == down_y, 1.0, 0.0).astype(jnp.bfloat16)


def fill_tables(lay, batch, cell, inverse, wx_hi, wx_lo, wy_hi, wy_lo):
    pick_sub = iota((PICK, LANES), 0).astype(jnp.float32)
    lat_sub = iota((lay.gy * CY, LANES), 0).astype(jnp.float32)

    def halves(value, high, low, at):
        top = value.astype(jnp.bfloat16)
        high[at] = top
        low[at] = (value - top.astype(jnp.float32)).astype(jnp.bfloat16)

    for c in range(lay.padded // LANES):
        lanes = slice(c * LANES, (c + 1) * LANES)
        start = c * LANES % lay.obs
        ox, oy = place_of(cell[batch : batch + 1, start : start + LANES], start, lay)
        halves(taper(jnp.abs(lat_sub - oy), inverse), wy_hi, wy_lo, (slice(None), lanes))
        for g in range(lay.gx):
            gap = jnp.abs(pick_sub + float(g * CX) - ox)
            gap = jnp.minimum(gap, jnp.abs(lay.extent - gap))
            halves(taper(gap, inverse), wx_hi, wx_lo, (slice(g * PICK, (g + 1) * PICK), lanes))


def tapers(lay, q, lanes, slots, pick_x, pick_y, wx_hi, wx_lo, wy_hi, wy_lo):
    at = slice(q * lay.block, (q + 1) * lay.block)
    near = slice(q * lay.pick_rows, (q + 1) * lay.pick_rows)

    def join(ref):
        return jnp.concatenate([ref[s, at, :] for s in slots], axis=0)

    by_x = dot(join(pick_x), jnp.concatenate([wx_hi[near, lanes], wx_lo[near, lanes]], axis=0))
    by_y = dot(join(pick_y), jnp.concatenate([wy_hi[:, lanes], wy_lo[:, lanes]], axis=0))
    return by_x * by_y


def table_shapes(lay, slots):
    half = jnp.bfloat16
    return [
        pltpu.VMEM((slots, lay.obs, 2 * lay.pick_rows), half),
        pltpu.VMEM((slots, lay.obs, 2 * lay.gy * CY), half),
        pltpu.VMEM((lay.gx * PICK, lay.padded), half),
        pltpu.VMEM((lay.gx * PICK, lay.padded), half),
        pltpu.VMEM((lay.gy * CY, lay.padded), half),
        pltpu.VMEM((lay.gy * CY, lay.padded), half),
    ]


def taper_kernel(lay, batch, later, radius, cell, w_ref, *scratch):
    pick_x, pick_y = scratch[:2]
    fill_picks(lay, later, cell, pick_x, pick_y, 0)
    fill_tables(lay, batch, cell, inverse_of(radius[batch]), *scratch[2:])
    reach = reach_of(radius[batch])

    def windows(i, carry):
        for q in range(lay.blocks):
            lanes = lay.place((q + i) * lay.per_block - reach)[0]
            w_ref[q, i] = tapers(lay, q, lanes, [0], *scratch).astype(jnp.bfloat16)
        return carry

    lax.fori_loop(0, lay.window_count(reach), windows, 0)


def sweep_kernel(lay, members, masks, pairs, radius, cell, error, *refs):
    parts = len(masks)
    n_w = len(pairs)
    gathered, z_in, stored, out_ref = refs[:parts], refs[parts], refs[parts + 1 : parts + 1 + n_w], refs[parts + 1 + n_w]
    z, cells, rows, obs_cells, hp, rhs, line = refs[parts + 2 + n_w :][:7]
    scratch = refs[parts + 2 + n_w :][7:]
    stored = dict(zip(pairs, stored))
    gx, gy = lax.axis_index("gx"), lax.axis_index("gy")
    batches = lay.batches
    packed = 2 * OBS_DEV

    wide = iota((OBS_DEV, LANES), 1)
    for part, owners in zip(gathered, masks):
        for i, (mx, my) in enumerate(owners):
            owner = (gx ^ mx) * lay.gy + (gy ^ my)
            at = pl.ds(pl.multiple_of(owner * OBS_DEV, OBS_DEV), OBS_DEV)
            a = part[i * packed : i * packed + OBS_DEV, :]
            b = part[i * packed + OBS_DEV : (i + 1) * packed, :]
            rows[0, at, :] = a
            rows[1, at, :] = b
            rows[2, at, :] = jnp.where(wide < SPILL, pltpu.roll(a, SPILL, 1), pltpu.roll(b, 2 * SPILL, 1))

    sub8 = iota((8, LANES), 0)
    lane = iota((LANES, LANES), 1)
    latitude = (iota((COLUMN, lay.block), 0) // LEVELS).astype(jnp.float32)

    def prepare(b, start):
        at = slice(start, start + LANES)
        block = rows[b, at, :]
        turned = block.T
        pert = turned[:members]
        err = error[b : b + 1, at]
        var = jnp.sum(pert * pert, axis=0, keepdims=True) * (1.0 / (members - 1))
        scale = 1.0 / ((members - 1) * (var + err))
        zeros = jnp.zeros((LANES - members, LANES), jnp.bfloat16)
        left = jnp.concatenate([pert.astype(jnp.bfloat16), zeros], axis=0)
        spread = jnp.where(lane < members, block, 0.0)
        var = jnp.sum(spread * spread, axis=1, keepdims=True) * (1.0 / (members - 1))
        err = block[:, ERR : ERR + 1]
        shrink = 1.0 / (1.0 + jnp.sqrt(err / (var + err)))
        right = jnp.where(lane == MEAN, block, shrink * spread).astype(jnp.bfloat16)
        ox, oy = place_of(cell[b : b + 1, at], start, lay)
        for slot, shift in ((start, 0.0), (lay.obs + start, lay.extent)):
            if slot < lay.padded:
                hp[:, slot : slot + LANES] = left
                rhs[slot : slot + LANES, :] = right
                line[:, slot : slot + LANES] = jnp.where(sub8 == 0, ox + shift, jnp.where(sub8 == 1, oy, scale))

    z[...] = z_in[...]
    for b in range(batches):
        reach = reach_of(radius[b])
        inverse = inverse_of(radius[b])
        for g in range(lay.obs // LANES):
            prepare(b, g * LANES)
        cells[...] = z[...].astype(jnp.bfloat16)

        def own_window(i, carry):
            lanes, shift = lay.place(gx - reach + i * lay.per_block)
            pert, right = hp[:, lanes], rhs[lanes, :]
            ox, oy, scale = line[0:1, lanes], line[1:2, lanes], line[2:3, lanes]
            by_row = taper(jnp.abs(latitude + (gy * CY).astype(jnp.float32) - oy), inverse) * scale
            for first in range(0, CX, COLUMNS):
                at = slice(first * COLUMN, (first + COLUMNS) * COLUMN)
                cov = dot(cells[at, :], pert)
                gains = []
                for x in range(COLUMNS):
                    here_x = (gx * CX + first + x).astype(jnp.float32) + shift
                    weight = taper(jnp.abs(here_x - ox), inverse) * by_row
                    gains.append((cov[x * COLUMN : (x + 1) * COLUMN] * weight).astype(jnp.bfloat16))
                z[at, :] = z[at, :] - dot(jnp.concatenate(gains, axis=0), right)
            return carry

        later = range(b + 1, batches)
        for nb in later:
            obs_cells[nb] = rows[nb].astype(jnp.bfloat16)
        if later and not lay.stored:
            for nb in later:
                fill_picks(lay, nb, cell, scratch[0], scratch[1], nb)
            fill_tables(lay, b, cell, inverse, *scratch[2:])

        def group_windows(i, carry):
            for q in range(lay.blocks):
                at = slice(q * lay.block, (q + 1) * lay.block)
                lanes = lay.place((q + i) * lay.per_block - reach)[0]
                if lay.stored:
                    weight = jnp.concatenate([stored[b, nb][q, i] for nb in later], axis=0).astype(jnp.float32)
                else:
                    weight = tapers(lay, q, lanes, later, *scratch)
                cov = dot(jnp.concatenate([obs_cells[nb, at, :] for nb in later], axis=0), hp[:, lanes])
                gain = (weight * line[2:3, lanes] * cov).astype(jnp.bfloat16)
                step = dot(gain, rhs[lanes, :])
                for n, nb in enumerate(later):
                    rows[nb, at, :] = rows[nb, at, :] - step[n * lay.block : (n + 1) * lay.block]
            return carry

        lax.fori_loop(0, (2 * reach + lay.per_block) // lay.per_block, own_window, 0)
        if later:
            lax.fori_loop(0, lay.window_count(reach), group_windows, 0)

    for x in range(CX):
        t = z[x * COLUMN : (x + 1) * COLUMN, :].T
        out_ref[pl.ds(x, members, stride=CX), :] = t[:members] + t[MEAN : MEAN + 1]


def exchange(rows, lay, cell, work):
    def send(held, masks, mx, my):
        n = lay.gx * lay.gy
        pairs = [(i, (i // lay.gy ^ mx) * lay.gy + (i % lay.gy ^ my)) for i in range(n)]
        other = lax.ppermute(held, ("gx", "gy"), pairs)
        return other, [(a ^ mx, b ^ my) for a, b in masks]

    gx_bits = [1 << i for i in range(lay.gx.bit_length() - 1)]
    gy_bits = [1 << i for i in range(lay.gy.bit_length() - 1)]
    masks = [(0, 0)]
    done = []
    steps = [(bit, 0) for bit in reversed(gx_bits[1:])] + [(0, bit) for bit in reversed(gy_bits[2:])]
    for step, (mx, my) in enumerate(steps):
        other, moved = send(rows, masks, mx, my)
        if step < len(work) - 1:
            beside = [f(cell) for f in work[step]]
            other, beside = lax.optimization_barrier((other, beside))
            done += beside
        rows, masks = jnp.concatenate([rows, other], axis=0), masks + moved
        rows, cell = lax.optimization_barrier((rows, cell))
    pieces = [(rows, masks)]
    pieces += [send(rows, masks, 0, my) for my in range(1, min(4, lay.gy))]
    arrived, beside = lax.optimization_barrier(([p for p, _ in pieces[1:]], [f(cell) for f in work[-1]]))
    pieces[1:] = [(p, m) for p, (_, m) in zip(arrived, pieces[1:])]
    done += beside
    pieces += [send(held, owners, bit, 0) for bit in gx_bits[:1] for held, owners in pieces]
    return [p for p, _ in pieces], [m for _, m in pieces], done


def per_device(gx_count, gy_count, ensemble, obs_values, obs_error, obs_cell, band_offsets):
    members, rows_here, row_len = ensemble.shape
    batches = obs_cell.shape[0]
    lay = Layout(gx_count, gy_count, batches)
    total = rows_here * row_len
    smem = pl.BlockSpec(memory_space=pltpu.SMEM)
    vmem = pl.BlockSpec(memory_space=pltpu.VMEM)
    hbm = pl.BlockSpec(memory_space=pl.ANY)
    params = pltpu.CompilerParams(vmem_limit_bytes=VMEM_LIMIT if lay.stored else None)
    flat = ensemble.reshape(members * rows_here, row_len)
    f32, bf16 = jnp.float32, jnp.bfloat16

    def cost(us):
        return pl.CostEstimate(flops=int(us * 1.0e9), bytes_accessed=int(us * 1e5), transcendentals=0)

    own = pl.pallas_call(
        functools.partial(pick_kernel, lay, members),
        out_shape=jax.ShapeDtypeStruct((2 * OBS_DEV, LANES), f32),
        in_specs=[hbm, hbm, hbm, hbm],
        out_specs=vmem,
        scratch_shapes=[
            pltpu.VMEM((total, LANES), f32),
            pltpu.VMEM(flat.shape, f32),
            pltpu.SMEM(obs_cell.shape, jnp.int32),
            pltpu.SMEM(obs_cell.shape, f32),
            pltpu.SMEM(obs_cell.shape, f32),
            pltpu.VMEM((batches * OBS_DEV, LANES), f32),
            pltpu.SemaphoreType.DMA((3 + PIECES,)),
        ],
        compiler_params=pltpu.CompilerParams(vmem_limit_bytes=PICK_LIMIT),
        cost_estimate=cost(2.0),
        name="pick",
    )(obs_cell, obs_error, obs_values, flat)

    def turn(unused):
        return pl.pallas_call(
            functools.partial(turn_kernel, members),
            out_shape=jax.ShapeDtypeStruct((total, LANES), f32),
            in_specs=[vmem],
            out_specs=vmem,
            compiler_params=params,
            cost_estimate=cost(0.5),
            name="turn",
        )(flat)

    def taper_of(b, later):
        return lambda cells: pl.pallas_call(
            functools.partial(taper_kernel, lay, b, later),
            out_shape=jax.ShapeDtypeStruct((lay.blocks, lay.windows, lay.block, lay.block), bf16),
            in_specs=[smem, vmem],
            out_specs=vmem,
            scratch_shapes=table_shapes(lay, 1),
            compiler_params=params,
            cost_estimate=cost(2.5),
            name="tapers",
        )(band_offsets, cells)

    pairs = [(b, later) for b in range(batches) for later in range(b + 1, batches)] if lay.stored else []
    work = [[taper_of(*pair)] for pair in pairs] or [[]]
    work[-1] = work[-1] + [turn]
    parts, masks, (*stored, z) = exchange(own, lay, obs_cell, work)
    out = pl.pallas_call(
        functools.partial(sweep_kernel, lay, members, masks, pairs),
        out_shape=jax.ShapeDtypeStruct((members * rows_here, row_len), f32),
        in_specs=[smem] + [vmem] * (3 + len(parts) + len(stored)),
        out_specs=vmem,
        scratch_shapes=[
            pltpu.VMEM((total, LANES), f32),
            pltpu.VMEM((total, LANES), bf16),
            pltpu.VMEM((batches, lay.obs, LANES), f32),
            pltpu.VMEM((batches, lay.obs, LANES), bf16),
            pltpu.VMEM((LANES, lay.padded), bf16),
            pltpu.VMEM((lay.padded, LANES), bf16),
            pltpu.VMEM((8, lay.padded), f32),
        ]
        + ([] if lay.stored else table_shapes(lay, batches)),
        compiler_params=params,
        cost_estimate=cost(15.0),
        name="sweep",
    )(band_offsets, obs_cell, obs_error, *parts, z, *stored)
    return out.reshape(ensemble.shape)


def solution(mesh):
    in_specs = (P(None, "gx", "gy"), P(), P(), P(), P())
    out_specs = P(None, "gx", "gy")
    body = functools.partial(per_device, mesh.shape["gx"], mesh.shape["gy"])
    return jax.shard_map(
        body, mesh=mesh, in_specs=in_specs, out_specs=out_specs, check_vma=False
    )
```

time: 313 us -> 47.5 us (0.15)
  blocking collectives: 208 us -> 0 us
  local copies, waits for them, and re-layouts: 51.6 us -> 0.27 us
  matrix products: 44.8 us -> 0 us
  Pallas kernels: 0 us -> 32.6 us
  starting transfers between devices: 0 us -> 9.82 us
  other arithmetic: 5.49 us -> 0.02 us
  waiting for transfers between devices: 0 us -> 4.99 us
    all_gather x3 -> x0, blocking collectives: 208 us -> none  [collect(): panel_now = lax.all_gather(prior_now, ('gx', 'gy'), axis=1, tiled=True)]
    dot_general x9 -> x0, matrix products: 44.8 us -> none  [update_cells(): lax.dot_general(weighted, gain_wts, (((1,), (1,)), ((), ())), preferred_e...]
    gather x12 -> x0, local copies, waits for them, and re-layouts: 42.4 us -> none  [the longest x3 13.6 us: per_device(): prepare_cell_ids = jnp.take(obs_cell[batch_id], obs_index)]
    pallas_call x0 -> x6, Pallas kernels: none -> 32.6 us  [the longest x1 19.9 us: per_device(): pl.pallas_call(functools.partial(sweep_kernel, lay, members, masks, pairs...]
    ppermute x0 -> x9, starting transfers between devices: none -> 9.82 us  [send(): other = lax.ppermute(held, ('gx', 'gy'), pairs)]
    ppermute x0 -> x9, waiting for transfers between devices: none -> 4.99 us  [send(): other = lax.ppermute(held, ('gx', 'gy'), pairs)]
    unnamed x20 -> x10, local copies, waits for them, and re-layouts: 3.82 us -> 0.27 us
  transfers between devices with their start and end apart: 0 -> 9, of which waited for: 0 -> 6; matrix products, arithmetic and copies ran while one was open for 0% -> 0% of each run, Pallas kernels for 0% -> 20%
where the time goes in v2:
time: 47.5 us; the launch traced here: 47.8 us
  Pallas kernels  32.6 us (69%)
  starting transfers between devices  9.82 us (21%)
  waiting for transfers between devices  4.99 us (11%)
    pallas_call x1, Pallas kernels, per_device(): pl.pallas_call(functools.partial(sweep_kernel, lay, members, masks, pairs...  19.9 us
    ppermute x9, starting transfers between devices, send(): other = lax.ppermute(held, ('gx', 'gy'), pairs)  9.82 us
    pallas_call x3, Pallas kernels, taper_of(): pl.pallas_call(functools.partial(taper_kernel, lay, b, later), out_shape=...  9.27 us
    ppermute x9, waiting for transfers between devices, send(): other = lax.ppermute(held, ('gx', 'gy'), pairs)  4.99 us
    pallas_call x1, Pallas kernels, per_device(): pl.pallas_call(functools.partial(pick_kernel, lay, members), out_shape=ja...  2.96 us
  transfers between devices with their start and end apart: 9, of which 6 were waited for; matrix products, arithmetic and copies ran while one was open for 0% of the time, Pallas kernels for 20%

profile of v2, /device:TPU:0, one launch (start us, length us, event | category | flops | bytes accessed | tf_op | source)
XLA Modules:
  0.0 47.8 jit_solution(12298490170362096913)
XLA Ops:
  0.0 3.0 %pick.1 = f32[64,128]{1,0:T(8,128)} custom-call(s32[3,1024]{1,0:T(4,128)} %cell.5, f32[3,1024]{1,0:T(4,128)} %error.1, f32[3,1024]{1,0:T(4,128)} %value_in.1, f32[1920,128]{1,0:T(8,128)} %bitcast.2), custom_call_target="tpu_custom_call" | custom-call | flops 2000000000 | bytes 200000 | tf_op jit(solution)/shard_map/pick/pallas_call | solution.py:342
  3.0 0.0 copy-start
  3.0 4.1 %collective-permute-start = (f32[64,128]{1,0:T(8,128)}, f32[64,128]{1,0:T(8,128)S(1)}, u32[]{:S(2)}, u32[]{:S(2)}) collective-permute-start(f32[64,128]{1,0:T(8,128)} %pick.1), channel_id=1, source_target_pairs={{0,16},{1,17},{2,18},{3,19},{4,20},{5,21},{6,22},{7,23},{8,24},{9,... | collective-permute-start | bytes 98312 | tf_op jit(solution)/shard_map/ppermute | solution.py:302
  7.1 3.4 %tapers.3.refs_9_ = bf16[4,4,256,256]{3,2,1,0:T(8,128)(2,1)S(1)} custom-call(s32[3]{0:T(128)S(1)} %copy-done.3, s32[3,1024]{1,0:T(4,128)S(1)} %copy-done.1), custom_call_target="tpu_custom_call" | custom-call | flops 2500000000 | bytes 250000 | tf_op jit(solution)/shard_map/tapers/pallas_call | solution.py:373
  10.5 0.0 copy-start.4
  10.5 0.5 %turn.1.refs_8_ = f32[3072,128]{1,0:T(8,128)S(1)} custom-call(f32[1920,128]{1,0:T(8,128)S(1)} %bitcast.3), custom_call_target="tpu_custom_call" | custom-call | flops 500000000 | bytes 50000 | tf_op jit(solution)/shard_map/turn/pallas_call | solution.py:362
  11.0 0.2 copy-done.4
  11.3 1.6 %collective-permute-start.1 = (f32[128,128]{1,0:T(8,128)S(1)}, f32[128,128]{1,0:T(8,128)S(1)}, u32[]{:S(2)}, u32[]{:S(2)}) collective-permute-start(f32[128,128]{1,0:T(8,128)S(1)} %pad_maximum_fusion.1), channel_id=1, source_target_pairs={{0,8},{1,9},{2,10},{3,11},{4,12},{5,13},{6,14},{7,15},{8,0},{9,1},... | collective-permute-start | bytes 196616 | tf_op jit(solution)/shard_map/ppermute | solution.py:302
  12.8 3.4 %tapers.4.refs_10_ = bf16[4,4,256,256]{3,2,1,0:T(8,128)(2,1)S(1)} custom-call(s32[3]{0:T(128)S(1)} %copy-done.3, s32[3,1024]{1,0:T(4,128)S(1)} %copy-done.1), custom_call_target="tpu_custom_call" | custom-call | flops 2500000000 | bytes 250000 | tf_op jit(solution)/shard_map/tapers/pallas_call | solution.py:373
  16.2 0.0 copy-start.2
  16.3 0.1 collective-permute-start.5
  16.3 2.5 %collective-permute-start.4 = (f32[256,128]{1,0:T(8,128)S(1)}, f32[256,128]{1,0:T(8,128)S(1)}, u32[]{:S(2)}, u32[]{:S(2)}) collective-permute-start(f32[256,128]{1,0:T(8,128)S(1)} %pad_maximum_fusion.refs_0_), channel_id=1, source_target_pairs={{0,3},{1,2},{2,1},{3,0},{4,7},{5,6},{6,5},{7,4},{8,11},{9,10},{10,... | collective-permute-start | bytes 393224 | tf_op jit(solution)/shard_map/ppermute | solution.py:302
  18.8 0.5 %collective-permute-start.3 = (f32[256,128]{1,0:T(8,128)S(1)}, f32[256,128]{1,0:T(8,128)S(1)}, u32[]{:S(2)}, u32[]{:S(2)}) collective-permute-start(f32[256,128]{1,0:T(8,128)S(1)} %pad_maximum_fusion.refs_0_), channel_id=1, source_target_pairs={{0,2},{1,3},{2,0},{3,1},{4,6},{5,7},{6,4},{7,5},{8,10},{9,11},{10,... | collective-permute-start | bytes 393224 | tf_op jit(solution)/shard_map/ppermute | solution.py:302
  19.4 0.5 %collective-permute-start.2 = (f32[256,128]{1,0:T(8,128)S(1)}, f32[256,128]{1,0:T(8,128)S(1)}, u32[]{:S(2)}, u32[]{:S(2)}) collective-permute-start(f32[256,128]{1,0:T(8,128)S(1)} %pad_maximum_fusion.refs_0_), channel_id=1, source_target_pairs={{0,1},{1,0},{2,3},{3,2},{4,5},{5,4},{6,7},{7,6},{8,9},{9,8},{10,11... | collective-permute-start | bytes 393224 | tf_op jit(solution)/shard_map/ppermute | solution.py:302
  19.9 2.5 %tapers.5.refs_11_ = bf16[4,4,256,256]{3,2,1,0:T(8,128)(2,1)S(1)} custom-call(s32[3]{0:T(128)S(1)} %copy-done.3, s32[3,1024]{1,0:T(4,128)S(1)} %copy-done.1), custom_call_target="tpu_custom_call" | custom-call | flops 2500000000 | bytes 250000 | tf_op jit(solution)/shard_map/tapers/pallas_call | solution.py:373
  22.4 1.0 %collective-permute-done.4.refs_3_ = f32[256,128]{1,0:T(8,128)S(1)} collective-permute-done((f32[256,128]{1,0:T(8,128)S(1)}, f32[256,128]{1,0:T(8,128)S(1)}, u32[]{:S(2)}, u32[]{:S(2)}) %collective-permute-start.4) | collective-permute-done | bytes 131104 | tf_op jit(solution)/shard_map/ppermute | solution.py:302
  23.4 2.5 %collective-permute-done.3.refs_2_ = f32[256,128]{1,0:T(8,128)S(1)} collective-permute-done((f32[256,128]{1,0:T(8,128)S(1)}, f32[256,128]{1,0:T(8,128)S(1)}, u32[]{:S(2)}, u32[]{:S(2)}) %collective-permute-start.3) | collective-permute-done | bytes 131104 | tf_op jit(solution)/shard_map/ppermute | solution.py:302
  26.0 0.1 collective-permute-done.2.refs_1_
  26.1 0.5 %collective-permute-start.7 = (f32[256,128]{1,0:T(8,128)S(1)}, f32[256,128]{1,0:T(8,128)S(1)}, u32[]{:S(2)}, u32[]{:S(2)}) collective-permute-start(f32[256,128]{1,0:T(8,128)S(1)} %collective-permute-done.3.refs_2_), channel_id=1, source_target_pairs={{0,4},{1,5},{2,6},{3,7},{4,0},{5,1},{6,2},{7,3},{8,12},{9,13},{10,... | collective-permute-start | bytes 393224 | tf_op jit(solution)/shard_map/ppermute | solution.py:302
  26.6 0.0 collective-permute-start.8
  26.6 0.8 %collective-permute-done.6.refs_5_ = f32[256,128]{1,0:T(8,128)S(1)} collective-permute-done((f32[256,128]{1,0:T(8,128)S(1)}, f32[256,128]{1,0:T(8,128)S(1)}, u32[]{:S(2)}, u32[]{:S(2)}) %collective-permute-start.6) | collective-permute-done | bytes 131104 | tf_op jit(solution)/shard_map/ppermute | solution.py:302
  27.4 0.2 collective-permute-done.7.refs_6_
  27.6 0.3 collective-permute-done.8.refs_7_
  27.9 19.9 %sweep.1 = f32[1920,128]{1,0:T(8,128)} custom-call(s32[3]{0:T(128)S(1)} %copy-done.3, s32[3,1024]{1,0:T(4,128)S(1)} %copy-done.1, f32[3,1024]{1,0:T(4,128)S(1)} %copy-done.2, f32[256,128]{1,0:T(8,128)S(1)} %pad_maximum_fusion.refs_0_, f32[256,128]{1,0:T(8,128)S(1)} %collective-permute-done.2.refs_1_, f32[256,128]{1,0:T(8,128)S(1)} %collective-permute-done.3.refs_2_, ...), custom_call_target="tpu_custom_call" | custom-call | flops 15000000512 | bytes 1500000 | tf_op jit(solution)/shard_map/sweep/pallas_call | solution.py:388
  (12 shorter events, 0.0 us)
Async XLA Ops:
  0.0 7.1 %copy-start.1 = (s32[3,1024]{1,0:T(4,128)S(1)}, s32[3,1024]{1,0:T(4,128)}, u32[]{:S(2)}) copy-start(s32[3,1024]{1,0:T(4,128)} %cell.5) | copy-start | bytes 36868
  0.0 7.1 %copy-start.3 = (s32[3]{0:T(128)S(1)}, s32[3]{0:T(128)}, u32[]{:S(2)}) copy-start(s32[3]{0:T(128)} %radius.7) | copy-start | bytes 40
  3.0 7.5 %copy-start = (f32[80,24,128]{2,1,0:T(8,128)S(1)}, f32[80,24,128]{2,1,0:T(8,128)}, u32[]{:S(2)}) copy-start(f32[80,24,128]{2,1,0:T(8,128)} %param.5) | copy-start | bytes 2949124
  3.0 8.0 %collective-permute-start = (f32[64,128]{1,0:T(8,128)}, f32[64,128]{1,0:T(8,128)S(1)}, u32[]{:S(2)}, u32[]{:S(2)}) collective-permute-start(f32[64,128]{1,0:T(8,128)} %pick.1), channel_id=1, source_target_pairs={{0,16},{1,17},{2,18},{3,19},{4,20},{5,21},{6,22},{7,23},{8,24},{9,... | collective-permute-start | bytes 98312 | tf_op jit(solution)/shard_map/ppermute | solution.py:302
  10.5 0.8 %copy-start.4 = (f32[64,128]{1,0:T(8,128)S(1)}, f32[64,128]{1,0:T(8,128)}, u32[]{:S(2)}) copy-start(f32[64,128]{1,0:T(8,128)} %pick.1) | copy-start | bytes 98308
  11.3 5.0 %collective-permute-start.1 = (f32[128,128]{1,0:T(8,128)S(1)}, f32[128,128]{1,0:T(8,128)S(1)}, u32[]{:S(2)}, u32[]{:S(2)}) collective-permute-start(f32[128,128]{1,0:T(8,128)S(1)} %pad_maximum_fusion.1), channel_id=1, source_target_pairs={{0,8},{1,9},{2,10},{3,11},{4,12},{5,13},{6,14},{7,15},{8,0},{9,1},... | collective-permute-start | bytes 196616 | tf_op jit(solution)/shard_map/ppermute | solution.py:302
  16.2 11.7 %copy-start.2 = (f32[3,1024]{1,0:T(4,128)S(1)}, f32[3,1024]{1,0:T(4,128)}, u32[]{:S(2)}) copy-start(f32[3,1024]{1,0:T(4,128)} %error.1) | copy-start | bytes 36868
  16.3 10.3 %collective-permute-start.5 = (f32[256,128]{1,0:T(8,128)S(1)}, f32[256,128]{1,0:T(8,128)S(1)}, u32[]{:S(2)}, u32[]{:S(2)}) collective-permute-start(f32[256,128]{1,0:T(8,128)S(1)} %pad_maximum_fusion.refs_0_), channel_id=1, source_target_pairs={{0,4},{1,5},{2,6},{3,7},{4,0},{5,1},{6,2},{7,3},{8,12},{9,13},{10,... | collective-permute-start | bytes 393224 | tf_op jit(solution)/shard_map/ppermute | solution.py:302
  16.3 7.1 %collective-permute-start.4 = (f32[256,128]{1,0:T(8,128)S(1)}, f32[256,128]{1,0:T(8,128)S(1)}, u32[]{:S(2)}, u32[]{:S(2)}) collective-permute-start(f32[256,128]{1,0:T(8,128)S(1)} %pad_maximum_fusion.refs_0_), channel_id=1, source_target_pairs={{0,3},{1,2},{2,1},{3,0},{4,7},{5,6},{6,5},{7,4},{8,11},{9,10},{10,... | collective-permute-start | bytes 393224 | tf_op jit(solution)/shard_map/ppermute | solution.py:302
  18.8 7.1 %collective-permute-start.3 = (f32[256,128]{1,0:T(8,128)S(1)}, f32[256,128]{1,0:T(8,128)S(1)}, u32[]{:S(2)}, u32[]{:S(2)}) collective-permute-start(f32[256,128]{1,0:T(8,128)S(1)} %pad_maximum_fusion.refs_0_), channel_id=1, source_target_pairs={{0,2},{1,3},{2,0},{3,1},{4,6},{5,7},{6,4},{7,5},{8,10},{9,11},{10,... | collective-permute-start | bytes 393224 | tf_op jit(solution)/shard_map/ppermute | solution.py:302
  19.4 6.7 %collective-permute-start.2 = (f32[256,128]{1,0:T(8,128)S(1)}, f32[256,128]{1,0:T(8,128)S(1)}, u32[]{:S(2)}, u32[]{:S(2)}) collective-permute-start(f32[256,128]{1,0:T(8,128)S(1)} %pad_maximum_fusion.refs_0_), channel_id=1, source_target_pairs={{0,1},{1,0},{2,3},{3,2},{4,5},{5,4},{6,7},{7,6},{8,9},{9,8},{10,11... | collective-permute-start | bytes 393224 | tf_op jit(solution)/shard_map/ppermute | solution.py:302
  26.1 1.3 %collective-permute-start.6 = (f32[256,128]{1,0:T(8,128)S(1)}, f32[256,128]{1,0:T(8,128)S(1)}, u32[]{:S(2)}, u32[]{:S(2)}) collective-permute-start(f32[256,128]{1,0:T(8,128)S(1)} %collective-permute-done.2.refs_1_), channel_id=1, source_target_pairs={{0,4},{1,5},{2,6},{3,7},{4,0},{5,1},{6,2},{7,3},{8,12},{9,13},{10,... | collective-permute-start | bytes 393224 | tf_op jit(solution)/shard_map/ppermute | solution.py:302
  26.1 1.5 %collective-permute-start.7 = (f32[256,128]{1,0:T(8,128)S(1)}, f32[256,128]{1,0:T(8,128)S(1)}, u32[]{:S(2)}, u32[]{:S(2)}) collective-permute-start(f32[256,128]{1,0:T(8,128)S(1)} %collective-permute-done.3.refs_2_), channel_id=1, source_target_pairs={{0,4},{1,5},{2,6},{3,7},{4,0},{5,1},{6,2},{7,3},{8,12},{9,13},{10,... | collective-permute-start | bytes 393224 | tf_op jit(solution)/shard_map/ppermute | solution.py:302
  26.6 1.3 %collective-permute-start.8 = (f32[256,128]{1,0:T(8,128)S(1)}, f32[256,128]{1,0:T(8,128)S(1)}, u32[]{:S(2)}, u32[]{:S(2)}) collective-permute-start(f32[256,128]{1,0:T(8,128)S(1)} %collective-permute-done.4.refs_3_), channel_id=1, source_target_pairs={{0,4},{1,5},{2,6},{3,7},{4,0},{5,1},{6,2},{7,3},{8,12},{9,13},{10,... | collective-permute-start | bytes 393224 | tf_op jit(solution)/shard_map/ppermute | solution.py:302
